TPU v7x, 32 devices: a whole 2x2x4 slice. The times are simulated.
32 devices in a mesh: clip: 2 (over x), tm: 4 (over z), chan: 4 (over y, core).
Axes of the slice: x: 2, y: 2, z: 4, core: 2. Of those that a mesh axis runs over, the one named last changes fastest.
Arguments:
- signal: bfloat16 [2, 4096, 256], P('clip', 'tm', 'chan'), may hold values from -6 to 6
- conv_first: bfloat16 [3, 256, 128], P(None, 'chan'), may hold values from -0.21875 to 0.21875
- conv_second: bfloat16 [128, 256], P(None, 'chan'), may hold values from -0.5 to 0.5
- conv_down: bfloat16 [16, 256, 512], P(None, 'chan'), may hold values from -0.09375 to 0.09375
- cotangent: bfloat16 [2, 512, 512], P('clip', 'tm'), may hold values from -6 to 6
Outputs:
- grad_signal: bfloat16 [2, 4096, 256], P('clip', 'tm', 'chan')
- grad_first: float32 [3, 256, 128], P(None, 'chan')
- grad_second: float32 [128, 256], P(None, 'chan')
- grad_down: float32 [16, 256, 512], P(None, 'chan')
All inputs are finite; a program needn't handle non-finite values.
Results may differ from a plain program's by a relative error of at most 0.018.
Values may be sent and summed in bfloat16 or wider, within the bound.
No kernel may reach another device: no remote copies, remote signals or barrier semaphores. Data moves between devices by JAX's collectives and lax.ppermute only.
A program may use at most 64 MiB of HBM per device.

v0:
```python
import jax
import jax.numpy as jnp
from jax import lax
from jax.sharding import PartitionSpec as P

KRES = 3
STRIDE = 8
RIM = 10


def shifted(block, axis, distance):
    devices = range(lax.axis_size(axis))
    route = [(i - distance, i) for i in devices if i - distance in devices]
    return lax.ppermute(block, axis, route)


def elu(value):
    return jnp.where(value > 0, value, jnp.exp(jnp.minimum(value, 0.0)) - 1.0)


def slope(value):
    return jnp.where(value > 0, 1.0, jnp.exp(jnp.minimum(value, 0.0)))


def contract_rows(left, right):
    return lax.dot_general(
        left, right, (((0,), (0,)), ((), ())), preferred_element_type=jnp.float32
    )


def contract_cols(left, right):
    return lax.dot_general(
        left, right, (((1,), (1,)), ((), ())), preferred_element_type=jnp.float32
    )


def causal_conv(values, weights, span):
    total = jnp.zeros((span, weights.shape[2]), jnp.float32)
    for k in range(KRES):
        total = total + jnp.dot(
            values[k : k + span], weights[k], preferred_element_type=jnp.float32
        )
    return total


def on_device(signal, conv_first, conv_second, conv_down, cotangent):
    frames = signal[0]
    length, local_ch = frames.shape
    span = length + RIM - KRES + 1
    borrowed = shifted(frames[length - RIM :], "tm", 1)
    padded = jnp.concatenate([borrowed, frames], axis=0)
    act = elu(padded.astype(jnp.float32)).astype(jnp.bfloat16)
    hidden = lax.psum(causal_conv(act, conv_first, span).astype(jnp.bfloat16), "chan").astype(
        jnp.float32
    )
    inner = elu(hidden).astype(jnp.bfloat16)
    resid = padded[KRES - 1 :].astype(jnp.float32) + jnp.dot(
        inner, conv_second, preferred_element_type=jnp.float32
    )
    feed = elu(resid).astype(jnp.bfloat16)
    blocks = feed.reshape(span // STRIDE, STRIDE * local_ch)
    wide = conv_down.reshape(2, STRIDE * local_ch, conv_down.shape[2])
    upstream = cotangent[0]
    count = upstream.shape[0]
    front = contract_cols(upstream, wide[0])
    back = contract_cols(upstream, wide[1])
    dblocks = jnp.pad(front, ((0, 1), (0, 0))) + jnp.pad(back, ((1, 0), (0, 0)))
    down_raw = jnp.stack(
        [contract_rows(blocks[:count], upstream), contract_rows(blocks[1:], upstream)]
    )
    down_raw = down_raw.reshape(conv_down.shape)
    dresid = dblocks.reshape(span, local_ch) * slope(resid)
    dres16 = dresid.astype(jnp.bfloat16)
    second_raw = contract_rows(inner, dres16)
    dinner = lax.psum(contract_cols(dres16, conv_second).astype(jnp.bfloat16), "chan").astype(
        jnp.float32
    )
    dhid = (dinner * slope(hidden)).astype(jnp.bfloat16)
    first_raw = jnp.stack([contract_rows(act[k : k + span], dhid) for k in range(KRES)])
    dact = jnp.zeros(padded.shape, jnp.float32)
    for k in range(KRES):
        dact = dact + jnp.pad(contract_cols(dhid, conv_first[k]), ((k, KRES - 1 - k), (0, 0)))
    dpadded = dact * slope(padded.astype(jnp.float32)) + jnp.pad(dresid, ((KRES - 1, 0), (0, 0)))
    returned = shifted(dpadded[:RIM], "tm", -1)
    grad_frames = dpadded[RIM:] + jnp.pad(returned, ((length - RIM, 0), (0, 0)))
    first_total, second_total, down_total = lax.psum(
        (first_raw, second_raw, down_raw), ("clip", "tm")
    )
    factor = 1.0 / jnp.sqrt(
        jnp.float32(lax.axis_size("clip") * lax.axis_size("tm") * (length // STRIDE))
    )
    return (
        grad_frames.astype(jnp.bfloat16)[None],
        first_total * factor,
        second_total * factor,
        down_total * factor,
    )


def solution(mesh):
    return jax.shard_map(
        on_device,
        mesh=mesh,
        in_specs=(
            P("clip", "tm", "chan"),
            P(None, "chan", None),
            P(None, "chan"),
            P(None, "chan", None),
            P("clip", "tm", None),
        ),
        out_specs=(
            P("clip", "tm", "chan"),
            P(None, "chan", None),
            P(None, "chan"),
            P(None, "chan", None),
        ),
        check_vma=False,
    )
```

profile of v0, /device:TPU:0, one launch (start us, length us, event | category | flops | bytes accessed | tf_op | source)
XLA Modules:
  0.0 208.7 jit_solution(13187131113075802272)
XLA Ops:
  7.2 0.9 slice_bitcast_fusion
  8.1 4.9 %collective-permute-start = (bf16[10,64]{0,1:T(8,128)(2,1)S(1)}, bf16[10,64]{0,1:T(8,128)(2,1)S(1)}, u32[]{:S(2)}, u32[]{:S(2)}) collective-permute-start(bf16[10,64]{0,1:T(8,128)(2,1)S(1)} %slice_bitcast_fusion), channel_id=1, source_target_pairs={{0,4},{4,8},{8,12},{1,5},{5,9},{9,13},{2,6},{6,10},{10,14},{3,7},{... | collective-permute-start | bytes 3848 | tf_op jit(solution)/shard_map/ppermute | solution.py:14
  13.0 1.3 fusion.56
  14.3 0.3 fusion.22
  14.8 0.3 fusion.29
  15.2 0.5 convolution_add_fusion.1
  15.6 1.2 fusion
  16.9 0.3 fusion.20
  17.6 32.4 %all-reduce.12.cloned.1.call-done = bf16[1032,128]{1,0:T(8,128)(2,1)} async-done(((bf16[1032,128]{1,0:T(8,128)(2,1)}), bf16[1032,128]{1,0:T(8,128)(2,1)}) %all-reduce.12.cloned.1.call-update) | async-done | bytes 264208 | tf_op jit(solution)/shard_map/psum | solution.py:53
  50.0 1.3 fusion.9
  52.2 1.0 convolution_convert_fusion
  53.3 0.3 convolution_bitcast_fusion
  53.6 0.3 convolution_bitcast_fusion.1
  54.0 1.5 pad_maximum_fusion
  55.4 30.2 %all-reduce.14.cloned.1.call-done = bf16[1032,128]{1,0:T(8,128)(2,1)} async-done(((bf16[1032,128]{1,0:T(8,128)(2,1)}), bf16[1032,128]{1,0:T(8,128)(2,1)}) %all-reduce.14.cloned.1.call-update) | async-done | bytes 264208 | tf_op jit(solution)/shard_map/psum | solution.py:75
  85.6 1.1 fusion.3
  86.7 0.2 convolution_bitcast_fusion.2
  87.0 0.2 convolution_bitcast_fusion.3
  87.4 0.7 pad_maximum_fusion.2
  88.1 0.3 fusion.31
  88.4 39.2 %psum.38 = f32[128,64]{0,1:T(8,128)S(1)} all-reduce(f32[128,64]{0,1:T(8,128)S(1)} %fusion.31), channel_id=1, replica_groups=mesh['clip'=2,'tm'=4,'chan'=4] {'clip','tm'}, use_global_device_ids=true, to_apply=%region_3.4 | all-reduce | flops 8192 | bytes 65536 | tf_op jit(solution)/shard_map/psum | solution.py:86
  127.6 0.2 fusion.37
  127.8 0.2 fusion.40
  128.0 0.2 fusion.43
  128.2 0.3 fusion.11
  128.6 1.3 collective-permute-start.1
  129.9 0.6 broadcast_multiply_fusion.2
  130.5 3.9 %collective-permute-done.1 = f32[10,64]{0,1:T(8,128)S(1)} collective-permute-done((f32[10,64]{0,1:T(8,128)S(1)}, f32[10,64]{0,1:T(8,128)S(1)}, u32[]{:S(2)}, u32[]{:S(2)}) %collective-permute-start.1) | collective-permute-done | bytes 2592 | tf_op jit(solution)/shard_map/ppermute | solution.py:14
  134.4 0.8 fusion.17
  135.2 62.3 %all-reduce.16.cloned.1.call-done = (f32[3,64,128]{2,1,0:T(8,128)}, f32[16,64,512]{2,1,0:T(8,128)}) async-done(((f32[3,64,128]{2,1,0:T(8,128)}, f32[16,64,512]{2,1,0:T(8,128)}), (f32[3,64,128]{2,1,0:T(8,128)}, f32[16,64,512]{2,1,0:T(8,128)})) %all-reduce.16.cloned.1.call-update) | async-done | bytes 2195472 | tf_op jit(solution)/shard_map/psum | solution.py:86
  197.5 1.5 broadcast_multiply_fusion.1
  199.0 3.2 %broadcast_multiply_fusion = f32[16,64,512]{2,1,0:T(8,128)} fusion(f32[16,64,512]{2,1,0:T(8,128)} %get-tuple-element.5), kind=kLoop, calls=%fused_computation.10 | loop fusion | flops 524288 | bytes 4194304 | tf_op jit(solution)/shard_map/mul | solution.py:96
  (28 shorter events, 1.8 us)
Async XLA Ops:
  7.2 7.2 %copy-start = (bf16[1,128,512]{2,1,0:T(8,128)(2,1)S(1)}, bf16[1,128,512]{2,1,0:T(8,128)(2,1)}, u32[]{:S(2)}) copy-start(bf16[1,128,512]{2,1,0:T(8,128)(2,1)} %param.9) | copy-start | bytes 393220
  7.2 7.5 %copy-start.1 = (bf16[1,1024,64]{1,2,0:T(8,128)(2,1)S(1)}, bf16[1,1024,64]{1,2,0:T(8,128)(2,1)}, u32[]{:S(2)}) copy-start(bf16[1,1024,64]{1,2,0:T(8,128)(2,1)} %param.5) | copy-start | bytes 393220
  7.2 7.6 %copy-start.3 = (bf16[3,64,128]{2,1,0:T(8,128)(2,1)S(1)}, bf16[3,64,128]{2,1,0:T(8,128)(2,1)}, u32[]{:S(2)}) copy-start(bf16[3,64,128]{2,1,0:T(8,128)(2,1)} %param.6) | copy-start | bytes 147460
  7.2 42.8 %all-reduce.12.cloned.1.call-start = ((), (), s32[]{:S(2)}) async-start(), calls=%async_computation | async-start | bytes 528384 | tf_op jit(solution)/shard_map/psum | solution.py:53
  8.1 6.5 %collective-permute-start = (bf16[10,64]{0,1:T(8,128)(2,1)S(1)}, bf16[10,64]{0,1:T(8,128)(2,1)S(1)}, u32[]{:S(2)}, u32[]{:S(2)}) collective-permute-start(bf16[10,64]{0,1:T(8,128)(2,1)S(1)} %slice_bitcast_fusion), channel_id=1, source_target_pairs={{0,4},{4,8},{8,12},{1,5},{5,9},{9,13},{2,6},{6,10},{10,14},{3,7},{... | collective-permute-start | bytes 3848 | tf_op jit(solution)/shard_map/ppermute | solution.py:14
  15.6 34.4 %copy-start.4 = (bf16[128,64]{0,1:T(8,128)(2,1)S(1)}, bf16[128,64]{0,1:T(8,128)(2,1)}, u32[]{:S(2)}) copy-start(bf16[128,64]{0,1:T(8,128)(2,1)} %param.7) | copy-start | bytes 49156
  16.8 68.8 %all-reduce.14.cloned.1.call-start = ((), (), s32[]{:S(2)}) async-start(), calls=%async_computation.1 | async-start | bytes 528384 | tf_op jit(solution)/shard_map/psum | solution.py:75
  53.3 144.2 %all-reduce.16.cloned.1.call-start = ((), (), s32[]{:S(2)}) async-start(), calls=%async_computation.2 | async-start | bytes 4390912 | tf_op jit(solution)/shard_map/psum | solution.py:86
  53.9 31.7 %copy-start.2 = (bf16[1032,128]{1,0:T(8,128)(2,1)S(1)}, bf16[1032,128]{1,0:T(8,128)(2,1)}, u32[]{:S(2)}) copy-start(bf16[1032,128]{1,0:T(8,128)(2,1)} %all-reduce.12.cloned.1.call-done) | copy-start | bytes 792580
  128.6 5.8 %collective-permute-start.1 = (f32[10,64]{0,1:T(8,128)S(1)}, f32[10,64]{0,1:T(8,128)S(1)}, u32[]{:S(2)}, u32[]{:S(2)}) collective-permute-start(f32[10,64]{0,1:T(8,128)S(1)} %slice.82), channel_id=1, source_target_pairs={{4,0},{8,4},{12,8},{5,1},{9,5},{13,9},{6,2},{10,6},{14,10},{7,3},{... | collective-permute-start | bytes 7688 | tf_op jit(solution)/shard_map/ppermute | solution.py:14
Sparse Core Ops, SparseCore 0:
  16.9 32.9 all-reduce.11
  53.4 32.2 all-reduce.13
  90.0 107.4 all-reduce.15
where the time goes:
time: 209 us
  waiting for transfers between devices  129 us (62%)
  blocking collectives  39.2 us (19%)
  between operations  13.9 us (7%)
  other arithmetic  9.89 us (5%)
  matrix products  7.15 us (3%)
  starting transfers between devices  6.33 us (3%)
  local copies, waits for them, and re-layouts  3.4 us (2%)
    psum x1, waiting for transfers between devices, on_device(): lax.psum((first_raw, second_raw, down_raw), ('clip', 'tm'))  62.3 us
    psum x1, blocking collectives, on_device(): lax.psum((first_raw, second_raw, down_raw), ('clip', 'tm'))  39.2 us
    psum x1, waiting for transfers between devices, on_device(): lax.psum(causal_conv(act, conv_first, span).astype(jnp.bfloat16), 'chan')  32.4 us
    psum x1, waiting for transfers between devices, on_device(): lax.psum(contract_cols(dres16, conv_second).astype(jnp.bfloat16), 'chan')  30.2 us
    ppermute x2, starting transfers between devices, shifted(): return lax.ppermute(block, axis, route)  6.21 us
  transfers between devices with their start and end apart: 5, of which 4 were waited for; matrix products, arithmetic and copies ran while one was open for 3% of the time, Pallas kernels for 0%

commit v1 on v0

--- a/solution.py
+++ b/solution.py
@@ -50,9 +50,9 @@
     borrowed = shifted(frames[length - RIM :], "tm", 1)
     padded = jnp.concatenate([borrowed, frames], axis=0)
     act = elu(padded.astype(jnp.float32)).astype(jnp.bfloat16)
-    hidden = lax.psum(causal_conv(act, conv_first, span).astype(jnp.bfloat16), "chan").astype(
-        jnp.float32
-    )
+    hidden = jnp.sum(
+        lax.all_gather(causal_conv(act, conv_first, span).astype(jnp.bfloat16), "chan"), 0
+    ).astype(jnp.float32)
     inner = elu(hidden).astype(jnp.bfloat16)
     resid = padded[KRES - 1 :].astype(jnp.float32) + jnp.dot(
         inner, conv_second, preferred_element_type=jnp.float32

time: 209 us -> 197 us (0.943)
  waiting for transfers between devices: 129 us -> 115 us
  other arithmetic: 9.89 us -> 12.3 us
    psum x1 -> x0, waiting for transfers between devices: 32.4 us -> none  [on_device(): lax.psum(causal_conv(act, conv_first, span).astype(jnp.bfloat16), 'chan')]
    all_gather x0 -> x1, waiting for transfers between devices: none -> 17.7 us  [on_device(): lax.all_gather(causal_conv(act, conv_first, span).astype(jnp.bfloat16), '...]
  transfers between devices with their start and end apart: 5 -> 5, of which waited for: 4 -> 5; matrix products, arithmetic and copies ran while one was open for 3% -> 3% of each run, Pallas kernels for 0% -> 0%
where the time goes in v1:
time: 197 us; the launch traced here: 196 us
  waiting for transfers between devices  115 us (58%)
  blocking collectives  39.2 us (20%)
  between operations  14 us (7%)
  other arithmetic  12.3 us (6%)
  matrix products  7.67 us (4%)
  starting transfers between devices  6.33 us (3%)
  local copies, waits for them, and re-layouts  2.24 us (1%)
    psum x1, waiting for transfers between devices, on_device(): lax.psum((first_raw, second_raw, down_raw), ('clip', 'tm'))  62.3 us
    psum x1, blocking collectives, on_device(): lax.psum((first_raw, second_raw, down_raw), ('clip', 'tm'))  39.2 us
    psum x1, waiting for transfers between devices, on_device(): lax.psum(contract_cols(dres16, conv_second).astype(jnp.bfloat16), 'chan')  29.2 us
    all_gather x1, waiting for transfers between devices, on_device(): lax.all_gather(causal_conv(act, conv_first, span).astype(jnp.bfloat16), '...  17.7 us
    ppermute x2, starting transfers between devices, shifted(): return lax.ppermute(block, axis, route)  6.21 us
    ppermute x2, waiting for transfers between devices, shifted(): return lax.ppermute(block, axis, route)  5.31 us
  transfers between devices with their start and end apart: 5, of which 5 were waited for; matrix products, arithmetic and copies ran while one was open for 3% of the time, Pallas kernels for 0%

profile of v1, /device:TPU:0, one launch (start us, length us, event | category | flops | bytes accessed | tf_op | source)
XLA Modules:
  0.0 196.2 jit_solution(17689625439678861433)
XLA Ops:
  7.2 0.9 slice_bitcast_fusion
  8.1 4.9 %collective-permute-start = (bf16[10,64]{0,1:T(8,128)(2,1)S(1)}, bf16[10,64]{0,1:T(8,128)(2,1)S(1)}, u32[]{:S(2)}, u32[]{:S(2)}) collective-permute-start(bf16[10,64]{0,1:T(8,128)(2,1)S(1)} %slice_bitcast_fusion), channel_id=1, source_target_pairs={{0,4},{4,8},{8,12},{1,5},{5,9},{9,13},{2,6},{6,10},{10,14},{3,7},{... | collective-permute-start | bytes 3848 | tf_op jit(solution)/shard_map/ppermute | solution.py:14
  13.1 1.4 collective-permute-done
  14.5 1.1 fusion.14
  15.5 1.1 fusion.29
  16.6 1.2 convolution_add_fusion.1
  17.8 1.2 fusion
  19.2 0.3 fusion.22
  19.5 0.3 fusion.20
  20.2 17.7 %all-gather.3.cloned.1.call-done = bf16[4128,128]{1,0:T(8,128)(2,1)} async-done(((bf16[1032,128]{1,0:T(8,128)(2,1)}), bf16[4128,128]{1,0:T(8,128)(2,1)}) %all-gather.3.cloned.1.call-update) | async-done | bytes 1056784 | tf_op jit(solution)/shard_map/all_gather | solution.py:54
  37.9 1.5 reduce_sum.12
  39.4 0.4 fusion.9
  40.7 1.0 convolution_convert_fusion
  41.8 0.3 convolution_bitcast_fusion
  42.1 0.3 convolution_bitcast_fusion.1
  42.4 1.5 pad_maximum_fusion
  43.9 29.2 %all-reduce.11.cloned.1.call-done = bf16[1032,128]{1,0:T(8,128)(2,1)} async-done(((bf16[1032,128]{1,0:T(8,128)(2,1)}), bf16[1032,128]{1,0:T(8,128)(2,1)}) %all-reduce.11.cloned.1.call-update) | async-done | bytes 264208 | tf_op jit(solution)/shard_map/psum | solution.py:75
  73.1 1.1 fusion.3
  74.2 0.2 convolution_bitcast_fusion.2
  74.5 0.2 convolution_bitcast_fusion.3
  74.9 0.7 pad_maximum_fusion.2
  75.6 0.3 fusion.31
  75.9 39.2 %psum.30 = f32[128,64]{0,1:T(8,128)S(1)} all-reduce(f32[128,64]{0,1:T(8,128)S(1)} %fusion.31), channel_id=1, replica_groups=mesh['clip'=2,'tm'=4,'chan'=4] {'clip','tm'}, use_global_device_ids=true, to_apply=%region_3.4 | all-reduce | flops 8192 | bytes 65536 | tf_op jit(solution)/shard_map/psum | solution.py:86
  115.5 0.2 fusion.43
  115.8 0.3 fusion.11
  116.1 1.3 collective-permute-start.1
  117.4 0.6 broadcast_multiply_fusion.2
  118.0 3.9 %collective-permute-done.1 = f32[10,64]{0,1:T(8,128)S(1)} collective-permute-done((f32[10,64]{0,1:T(8,128)S(1)}, f32[10,64]{0,1:T(8,128)S(1)}, u32[]{:S(2)}, u32[]{:S(2)}) %collective-permute-start.1) | collective-permute-done | bytes 2592 | tf_op jit(solution)/shard_map/ppermute | solution.py:14
  121.9 0.8 fusion.17
  122.7 62.3 %all-reduce.13.cloned.1.call-done = (f32[3,64,128]{2,1,0:T(8,128)}, f32[16,64,512]{2,1,0:T(8,128)}) async-done(((f32[3,64,128]{2,1,0:T(8,128)}, f32[16,64,512]{2,1,0:T(8,128)}), (f32[3,64,128]{2,1,0:T(8,128)}, f32[16,64,512]{2,1,0:T(8,128)})) %all-reduce.13.cloned.1.call-update) | async-done | bytes 2195472 | tf_op jit(solution)/shard_map/psum | solution.py:86
  185.0 1.5 broadcast_multiply_fusion.1
  186.5 3.2 %broadcast_multiply_fusion = f32[16,64,512]{2,1,0:T(8,128)} fusion(f32[16,64,512]{2,1,0:T(8,128)} %get-tuple-element.5), kind=kLoop, calls=%fused_computation.10 | loop fusion | flops 524288 | bytes 4194304 | tf_op jit(solution)/shard_map/mul | solution.py:96
  (29 shorter events, 2.2 us)
Async XLA Ops:
  7.2 12.0 %copy-start = (bf16[1,128,512]{2,1,0:T(8,128)(2,1)S(1)}, bf16[1,128,512]{2,1,0:T(8,128)(2,1)}, u32[]{:S(2)}) copy-start(bf16[1,128,512]{2,1,0:T(8,128)(2,1)} %param.9) | copy-start | bytes 393220
  7.2 10.6 %copy-start.3 = (bf16[3,64,128]{2,1,0:T(8,128)(2,1)S(1)}, bf16[3,64,128]{2,1,0:T(8,128)(2,1)}, u32[]{:S(2)}) copy-start(bf16[3,64,128]{2,1,0:T(8,128)(2,1)} %param.6) | copy-start | bytes 147460
  7.2 11.8 %copy-start.1 = (bf16[16,64,512]{2,1,0:T(8,128)(2,1)S(1)}, bf16[16,64,512]{2,1,0:T(8,128)(2,1)}, u32[]{:S(2)}) copy-start(bf16[16,64,512]{2,1,0:T(8,128)(2,1)} %param.8) | copy-start | bytes 3145732
  7.2 30.7 %all-gather.3.cloned.1.call-start = ((), (), s32[]{:S(2)}) async-start(), calls=%async_computation.1 | async-start | bytes 1320960 | tf_op jit(solution)/shard_map/all_gather | solution.py:54
  8.1 6.4 %collective-permute-start = (bf16[10,64]{0,1:T(8,128)(2,1)S(1)}, bf16[10,64]{0,1:T(8,128)(2,1)S(1)}, u32[]{:S(2)}, u32[]{:S(2)}) collective-permute-start(bf16[10,64]{0,1:T(8,128)(2,1)S(1)} %slice_bitcast_fusion), channel_id=1, source_target_pairs={{0,4},{4,8},{8,12},{1,5},{5,9},{9,13},{2,6},{6,10},{10,14},{3,7},{... | collective-permute-start | bytes 3848 | tf_op jit(solution)/shard_map/ppermute | solution.py:14
  19.0 54.1 %all-reduce.11.cloned.1.call-start = ((), (), s32[]{:S(2)}) async-start(), calls=%async_computation | async-start | bytes 528384 | tf_op jit(solution)/shard_map/psum | solution.py:75
  19.8 19.6 %copy-start.2 = (bf16[1,1024,64]{1,2,0:T(8,128)(2,1)S(1)}, bf16[1,1024,64]{1,2,0:T(8,128)(2,1)}, u32[]{:S(2)}) copy-start(bf16[1,1024,64]{1,2,0:T(8,128)(2,1)} %param.5) | copy-start | bytes 393220
  19.8 19.6 %copy-start.4 = (bf16[128,64]{0,1:T(8,128)(2,1)S(1)}, bf16[128,64]{0,1:T(8,128)(2,1)}, u32[]{:S(2)}) copy-start(bf16[128,64]{0,1:T(8,128)(2,1)} %param.7) | copy-start | bytes 49156
  41.7 143.3 %all-reduce.13.cloned.1.call-start = ((), (), s32[]{:S(2)}) async-start(), calls=%async_computation.2 | async-start | bytes 4390912 | tf_op jit(solution)/shard_map/psum | solution.py:86
  116.1 5.8 %collective-permute-start.1 = (f32[10,64]{0,1:T(8,128)S(1)}, f32[10,64]{0,1:T(8,128)S(1)}, u32[]{:S(2)}, u32[]{:S(2)}) collective-permute-start(f32[10,64]{0,1:T(8,128)S(1)} %slice.82), channel_id=1, source_target_pairs={{4,0},{8,4},{12,8},{5,1},{9,5},{13,9},{6,2},{10,6},{14,10},{7,3},{... | collective-permute-start | bytes 7688 | tf_op jit(solution)/shard_map/ppermute | solution.py:14
Sparse Core Ops, SparseCore 0:
  19.1 18.7 all-gather.2
  41.9 31.2 all-reduce.10
  77.5 107.4 all-reduce.12
